TPU v7x, 256 devices: a whole 4x4x8 slice. The times are simulated.
256 devices in a mesh: dp: 8 (over x, z_hi), pipe: 4 (over z_lo), expert: 8 (over y, core).
Axes of the slice: x: 4, y: 4, z: 8 (z_hi: 2, z_lo: 4; z = z_hi * 4 + z_lo), core: 2. Of those that a mesh axis runs over, the one named last changes fastest.
Arguments:
- tokens: bfloat16 [8192, 2048], P(('dp', 'expert')), may hold values from -6 to 6
- cotangent: bfloat16 [8192, 2048], P(('dp', 'expert')), may hold values from -6 to 6
- owner_ids: int32 [4, 8192, 4], P('pipe', ('dp', 'expert')), may hold values from 0 to 63, all different within a row; in each aligned block of 32 rows (0 to 31, 32 to 63, ..., all dimensions but the last counted through in order) at most 3 rows name the same one
- gate_weights: bfloat16 [4, 8192, 4], P('pipe', ('dp', 'expert')), may hold values from 0.049804688 to 0.25
- norm_gain: float32 [4, 2048], P('pipe'), may hold values from 0.5 to 1.5
- w_gate: bfloat16 [4, 64, 2048, 384], P('pipe', ('dp', 'expert')), may hold values from -0.125 to 0.125
- w_up: bfloat16 [4, 64, 2048, 384], P('pipe', ('dp', 'expert')), may hold values from -0.125 to 0.125
- w_down: bfloat16 [4, 64, 384, 2048], P('pipe', ('dp', 'expert')), may hold values from -0.3125 to 0.3125
Outputs:
- segment_out: bfloat16 [4, 8192, 2048], P('pipe', ('dp', 'expert'))
- segment_grad: bfloat16 [4, 8192, 2048], P('pipe', ('dp', 'expert'))
- gain_grad: float32 [4, 2048], P('pipe')
Inputs may be any that keep to these rules, and one draw needn't show every extreme that they name: `owner_ids`: each row names 4 different owners. In each aligned block of 32 rows (layers in order, then tokens) no owner is named by more than 3 rows, and that bound is reached.
All inputs are finite; a program needn't handle non-finite values.
Results may differ from a plain program's by a relative error of at most 0.014.
Values may be sent and summed in bfloat16 or wider, within the bound.
A program may use at most 128 MiB of HBM per device.

v0:
```python
import jax
import jax.numpy as jnp
from jax import lax
from jax.sharding import PartitionSpec as P

MICRO = 4
epsilon = 1e-06


def from_behind(value, axis, steps):
    count = lax.axis_size(axis)
    leading, last = (max(0, -steps), min(count, count - steps))
    return lax.ppermute(value, axis, [(source, source + steps) for source in range(leading, last)])


def inverse_rms(values):
    return lax.rsqrt(jnp.mean(values * values, axis=-1, keepdims=True) + epsilon)


def contract_last(left, right):
    return lax.dot_general(
        left, right, (((1,), (1,)), ((), ())), preferred_element_type=jnp.float32
    )


def route_tables(ids_part, owners, capacity):
    owner_range = jnp.arange(owners, dtype=jnp.int32)
    onehot = (ids_part[:, :, None] == owner_range[None, None, :]).astype(jnp.int32)
    member = jnp.sum(onehot, axis=1)
    position = jnp.cumsum(member, axis=0) - member
    slot_range = jnp.arange(capacity, dtype=jnp.int32)
    placed = (position[:, :, None] == slot_range[None, None, :]) & (member[:, :, None] > 0)
    placing = jnp.transpose(placed, (1, 2, 0)).astype(jnp.bfloat16)
    return (onehot.astype(jnp.float32), placing)


def gate_slots(onehot, gates_part, placing, experts_here):
    gate_pairs = gates_part.astype(jnp.float32).reshape(gates_part.shape[0], -1, experts_here)
    chosen = jnp.einsum("rjo,rjc->roc", onehot, gate_pairs)
    return jnp.einsum("okr,roc->okc", placing.astype(jnp.float32), chosen).astype(jnp.bfloat16)


def send_rows(row_block, pair_block):
    got_rows, got_pairs = (
        lax.all_to_all(row_block, ("dp", "expert"), split_axis=0, concat_axis=0, tiled=True),
        lax.all_to_all(pair_block, ("dp", "expert"), split_axis=0, concat_axis=0, tiled=True),
    )
    return (got_rows, got_pairs)


def return_rows(row_block):
    return lax.all_to_all(row_block, ("dp", "expert"), split_axis=0, concat_axis=0, tiled=True)


def send_grads(row_block):
    return lax.all_to_all(row_block, ("dp", "expert"), split_axis=0, concat_axis=0, tiled=True)


def return_grads(row_block):
    return lax.all_to_all(row_block, ("dp", "expert"), split_axis=0, concat_axis=0, tiled=True)


def expert_forward(flat_rows, flat_pairs, joint_mats, down_mats):
    hidden_width = down_mats.shape[1]
    joint_pre = jnp.dot(flat_rows, joint_mats[0], preferred_element_type=jnp.float32)
    gate_pre = joint_pre[:, :hidden_width]
    up_pre = joint_pre[:, hidden_width:]
    hidden = (jax.nn.silu(gate_pre) * up_pre).astype(jnp.bfloat16)
    projected = jnp.dot(hidden, down_mats[0], preferred_element_type=jnp.float32)
    term = flat_pairs.astype(jnp.float32) * projected
    kept_both = [joint_pre]
    return (term.astype(jnp.bfloat16), jnp.stack(kept_both))


def expert_backward(grad_rows, flat_pairs, joint_keep, joint_mats, down_mats):
    hidden_width = down_mats.shape[1]
    q_vals = contract_last(grad_rows, down_mats[0])
    gate_pre = joint_keep[0][:, :hidden_width]
    up_pre = joint_keep[0][:, hidden_width:]
    sigma = jax.nn.sigmoid(gate_pre)
    weight = flat_pairs.astype(jnp.float32)
    d_gate = (q_vals * weight * up_pre * sigma * (1.0 + gate_pre * (1.0 - sigma))).astype(
        jnp.bfloat16
    )
    d_up = (q_vals * weight * gate_pre * sigma).astype(jnp.bfloat16)
    joint_grad = jnp.concatenate([d_gate, d_up], axis=1)
    term = contract_last(joint_grad, joint_mats[0])
    return term.astype(jnp.bfloat16)


def body(tokens, cotangent, owner_ids, gate_weights, norm_gain, w_gate, w_up, w_down):
    segments = lax.axis_size("pipe")
    segment_index = lax.axis_index("pipe")
    owners = lax.axis_size("dp") * lax.axis_size("expert")
    tok_rows = tokens.shape[0]
    width = tokens.shape[1]
    micro_rows = tok_rows // MICRO
    route_count = owner_ids.shape[2]
    capacity = max(2, (5 * micro_rows * route_count + 4 * owners - 1) // (4 * owners))
    slot_count = owners * capacity
    gain_row = norm_gain[0]
    joint_mats = jnp.concatenate([w_gate[0], w_up[0]], axis=2)
    down_mats = w_down[0]
    layer_ids = owner_ids[0]
    layer_gates = gate_weights[0]
    experts_here = joint_mats.shape[0]
    joint_width = joint_mats.shape[2]

    def skip_forward(operands):
        return (
            jnp.zeros((slot_count, width), jnp.bfloat16),
            jnp.zeros((experts_here, slot_count, joint_width), jnp.float32),
        )

    def run_forward(operands):
        return expert_forward(operands[0], operands[1], joint_mats, down_mats)

    def skip_backward(operands):
        return jnp.zeros((slot_count, width), jnp.bfloat16)

    def run_backward(operands):
        return expert_backward(operands[0], operands[1], operands[2], joint_mats, down_mats)

    def timing(micro):
        is_valid = (micro >= 0) & (micro < MICRO)
        slot_pick = jnp.where(is_valid, micro, MICRO)
        start_row = jnp.clip(micro, 0, MICRO - 1) * micro_rows
        return (is_valid, slot_pick, start_row)

    layer_outs = jnp.zeros((MICRO + 1, micro_rows, width), jnp.bfloat16)
    layer_ins = jnp.zeros((MICRO + 1, micro_rows, width), jnp.bfloat16)
    kept_joint = jnp.zeros((MICRO + 1, experts_here, slot_count, joint_width), jnp.float32)
    kept_pairs = jnp.zeros((MICRO + 1, slot_count, experts_here), jnp.bfloat16)
    grad_outs = jnp.zeros((MICRO + 1, micro_rows, width), jnp.bfloat16)
    gain_sum = jnp.zeros((width,), jnp.float32)
    ticks = MICRO + segments - 1
    incoming = jnp.zeros((micro_rows, width), jnp.bfloat16)
    for tick_num in range(ticks):
        forward_is_valid, forward_slot_pick, forward_start_row = timing(tick_num - segment_index)
        forward_own_part = lax.dynamic_slice_in_dim(tokens, forward_start_row, micro_rows, 0)
        forward_layer_in = jnp.where(segment_index == 0, forward_own_part, incoming)
        forward_ids_part = lax.dynamic_slice_in_dim(layer_ids, forward_start_row, micro_rows, 0)
        gates_part = lax.dynamic_slice_in_dim(layer_gates, forward_start_row, micro_rows, 0)
        forward_x_float = forward_layer_in.astype(jnp.float32)
        forward_scale = inverse_rms(forward_x_float)
        normed = (forward_x_float * forward_scale * gain_row).astype(jnp.bfloat16)
        forward_onehot, forward_placing = route_tables(forward_ids_part, owners, capacity)
        row_block = jnp.einsum(
            "okr,rd->okd", forward_placing, normed, preferred_element_type=jnp.float32
        ).astype(jnp.bfloat16)
        pair_block = gate_slots(forward_onehot, gates_part, forward_placing, experts_here)
        f_valid, f_pick, layer_in, x_float, f_placing, row_block, pair_block = (
            forward_is_valid,
            forward_slot_pick,
            forward_layer_in,
            forward_x_float,
            forward_placing,
            row_block,
            pair_block,
        )
        got_rows, got_pairs = send_rows(row_block, pair_block)
        flat_rows = got_rows.reshape(slot_count, width)
        flat_pairs = got_pairs.reshape(slot_count, experts_here)
        result, joint_pre = lax.cond(f_valid, run_forward, skip_forward, (flat_rows, flat_pairs))
        returned = return_rows(result.reshape(owners, capacity, width))
        branch = jnp.einsum("okr,okd->rd", f_placing, returned, preferred_element_type=jnp.float32)
        layer_out = (x_float + branch).astype(jnp.bfloat16)
        layer_outs = lax.dynamic_update_index_in_dim(layer_outs, layer_out, f_pick, 0)
        layer_ins = lax.dynamic_update_index_in_dim(layer_ins, layer_in, f_pick, 0)
        kept_joint = lax.dynamic_update_index_in_dim(kept_joint, joint_pre, f_pick, 0)
        kept_pairs = lax.dynamic_update_index_in_dim(kept_pairs, flat_pairs, f_pick, 0)
        if tick_num + 1 < ticks:
            incoming = from_behind(layer_out, "pipe", 1)
    incoming = jnp.zeros((micro_rows, width), jnp.bfloat16)
    for tick_num in range(ticks):
        backward_is_valid, backward_slot_pick, backward_start_row = timing(
            tick_num - (segments - 1 - segment_index)
        )
        own_part = lax.dynamic_slice_in_dim(cotangent, backward_start_row, micro_rows, 0)
        backward_grad_in = jnp.where(segment_index == segments - 1, own_part, incoming)
        ids_part = lax.dynamic_slice_in_dim(layer_ids, backward_start_row, micro_rows, 0)
        backward_layer_in = lax.dynamic_index_in_dim(
            layer_ins, backward_slot_pick, 0, keepdims=False
        )
        backward_x_float = backward_layer_in.astype(jnp.float32)
        backward_scale = inverse_rms(backward_x_float)
        onehot, backward_placing = route_tables(ids_part, owners, capacity)
        grad_block = jnp.einsum(
            "okr,rd->okd", backward_placing, backward_grad_in, preferred_element_type=jnp.float32
        ).astype(jnp.bfloat16)
        b_valid, b_pick, grad_in, bx_float, b_scale, b_placing, grad_block = (
            backward_is_valid,
            backward_slot_pick,
            backward_grad_in,
            backward_x_float,
            backward_scale,
            backward_placing,
            grad_block,
        )
        got_grads = send_grads(grad_block).reshape(slot_count, width)
        joint_keep = lax.dynamic_index_in_dim(kept_joint, b_pick, 0, keepdims=False)
        pair_keep = lax.dynamic_index_in_dim(kept_pairs, b_pick, 0, keepdims=False)
        owner_grad = lax.cond(
            b_valid, run_backward, skip_backward, (got_grads, pair_keep, joint_keep)
        )
        returned = return_grads(owner_grad.reshape(owners, capacity, width))
        normed_grad = jnp.einsum(
            "okr,okd->rd", b_placing, returned, preferred_element_type=jnp.float32
        )
        weighted = gain_row * normed_grad
        grad_x = (
            grad_in.astype(jnp.float32)
            + b_scale * weighted
            - bx_float
            * b_scale
            * b_scale
            * b_scale
            * jnp.mean(weighted * bx_float, axis=-1, keepdims=True)
        )
        gain_term = jnp.where(b_valid, jnp.sum(normed_grad * bx_float * b_scale, axis=0), 0.0)
        grad_bf, gain_term = (grad_x.astype(jnp.bfloat16), gain_term)
        grad_outs = lax.dynamic_update_index_in_dim(grad_outs, grad_bf, b_pick, 0)
        gain_sum = gain_sum + gain_term
        if tick_num + 1 < ticks:
            incoming = from_behind(grad_bf, "pipe", -1)
    gain_grad = lax.psum(gain_sum, ("dp", "expert"))
    segment_out = layer_outs[:MICRO].reshape(1, tok_rows, width)
    segment_grad = grad_outs[:MICRO].reshape(1, tok_rows, width)
    return (segment_out, segment_grad, gain_grad.reshape(1, width))


def solution(mesh):
    in_specs = (
        P(("dp", "expert"), None),
        P(("dp", "expert"), None),
        P("pipe", ("dp", "expert"), None),
        P("pipe", ("dp", "expert"), None),
        P("pipe", None),
        P("pipe", ("dp", "expert"), None, None),
        P("pipe", ("dp", "expert"), None, None),
        P("pipe", ("dp", "expert"), None, None),
    )
    out_specs = (
        P("pipe", ("dp", "expert"), None),
        P("pipe", ("dp", "expert"), None),
        P("pipe", None),
    )
    return jax.shard_map(body, mesh=mesh, in_specs=in_specs, out_specs=out_specs, check_vma=False)
```

profile of v0, /device:TPU:1, one launch (start us, length us, event | category | flops | bytes accessed | tf_op | source)
XLA Modules:
  0.0 1507.8 jit_solution(17595029229092546663)
XLA Ops:
  5.5 15.6 %all-to-all-start = ((bf16[64,3,1]{1,2,0:T(2,128)(2,1)}), bf16[64,3,1]{1,2,0:T(2,128)(2,1)S(1)}, u32[]{:S(2)}, u32[]{:S(2)}) async-start(bf16[64,3,1]{1,2,0:T(2,128)(2,1)} %copy.214), calls=%async_computation | async-start | bytes 65536 | tf_op jit(solution)/shard_map/all_to_all | solution.py:46
  40.4 25.5 %all-to-all-done.1 = bf16[64,3,2048]{2,1,0:T(4,128)(2,1)} async-done(((bf16[64,3,2048]{2,1,0:T(4,128)(2,1)}), bf16[64,3,2048]{2,1,0:T(4,128)(2,1)}, u32[]{:S(2)}, u32[]{:S(2)}) %all-to-all-start.1) | async-done | bytes 786464 | tf_op jit(solution)/shard_map/all_to_all | solution.py:45
  65.9 9.1 conditional.14
  84.8 18.1 %all-to-all-done.2 = bf16[64,3,2048]{2,1,0:T(4,128)(2,1)} async-done(((bf16[64,3,2048]{2,1,0:T(4,128)(2,1)}), bf16[64,3,2048]{2,1,0:T(4,128)(2,1)}, u32[]{:S(2)}, u32[]{:S(2)}) %all-to-all-start.2) | async-done | bytes 786464 | tf_op jit(solution)/shard_map/all_to_all | solution.py:52
  122.4 14.5 all-to-all-start.4
  136.9 28.5 %all-to-all-done.4 = bf16[64,3,2048]{2,1,0:T(4,128)(2,1)} async-done(((bf16[64,3,2048]{2,1,0:T(4,128)(2,1)}), bf16[64,3,2048]{2,1,0:T(4,128)(2,1)}, u32[]{:S(2)}, u32[]{:S(2)}) %all-to-all-start.4) | async-done | bytes 786464 | tf_op jit(solution)/shard_map/all_to_all | solution.py:45
  165.4 9.3 conditional.15
  184.1 18.4 %all-to-all-done.5 = bf16[64,3,2048]{2,1,0:T(4,128)(2,1)} async-done(((bf16[64,3,2048]{2,1,0:T(4,128)(2,1)}), bf16[64,3,2048]{2,1,0:T(4,128)(2,1)}, u32[]{:S(2)}, u32[]{:S(2)}) %all-to-all-start.5) | async-done | bytes 786464 | tf_op jit(solution)/shard_map/all_to_all | solution.py:52
  205.4 17.4 %collective-permute-start.1 = (bf16[32,2048]{1,0:T(8,128)(2,1)S(1)}, bf16[32,2048]{1,0:T(8,128)(2,1)S(1)}, u32[]{:S(2)}, u32[]{:S(2)}) collective-permute-start(bf16[32,2048]{1,0:T(8,128)(2,1)S(1)} %get-tuple-element.841), channel_id=1, source_target_pairs={{0,8},{8,16},{16,24},{1,9},{9,17},{17,25},{2,10},{10,18},{18,26},{... | collective-permute-start | bytes 393224 | tf_op jit(solution)/shard_map/ppermute | solution.py:13
  246.7 28.6 %all-to-all-done.7 = bf16[64,3,2048]{2,1,0:T(4,128)(2,1)} async-done(((bf16[64,3,2048]{2,1,0:T(4,128)(2,1)}), bf16[64,3,2048]{2,1,0:T(4,128)(2,1)}, u32[]{:S(2)}, u32[]{:S(2)}) %all-to-all-start.7) | async-done | bytes 786464 | tf_op jit(solution)/shard_map/all_to_all | solution.py:45
  275.3 9.1 conditional.16
  298.6 20.2 %all-to-all-done.8 = bf16[64,3,2048]{2,1,0:T(4,128)(2,1)} async-done(((bf16[64,3,2048]{2,1,0:T(4,128)(2,1)}), bf16[64,3,2048]{2,1,0:T(4,128)(2,1)}, u32[]{:S(2)}, u32[]{:S(2)}) %all-to-all-start.8) | async-done | bytes 786464 | tf_op jit(solution)/shard_map/all_to_all | solution.py:52
  324.2 9.3 all-to-all-start.9
  350.9 26.9 %all-to-all-done.10 = bf16[64,3,2048]{2,1,0:T(4,128)(2,1)} async-done(((bf16[64,3,2048]{2,1,0:T(4,128)(2,1)}), bf16[64,3,2048]{2,1,0:T(4,128)(2,1)}, u32[]{:S(2)}, u32[]{:S(2)}) %all-to-all-start.10) | async-done | bytes 786464 | tf_op jit(solution)/shard_map/all_to_all | solution.py:45
  377.8 9.1 conditional.17
  390.2 9.2 all-to-all-start.11
  399.7 21.5 %all-to-all-done.11 = bf16[64,3,2048]{2,1,0:T(4,128)(2,1)} async-done(((bf16[64,3,2048]{2,1,0:T(4,128)(2,1)}), bf16[64,3,2048]{2,1,0:T(4,128)(2,1)}, u32[]{:S(2)}, u32[]{:S(2)}) %all-to-all-start.11) | async-done | bytes 786464 | tf_op jit(solution)/shard_map/all_to_all | solution.py:52
  426.2 9.1 all-to-all-start.12
  452.8 21.8 %all-to-all-done.13 = bf16[64,3,2048]{2,1,0:T(4,128)(2,1)} async-done(((bf16[64,3,2048]{2,1,0:T(4,128)(2,1)}), bf16[64,3,2048]{2,1,0:T(4,128)(2,1)}, u32[]{:S(2)}, u32[]{:S(2)}) %all-to-all-start.13) | async-done | bytes 786464 | tf_op jit(solution)/shard_map/all_to_all | solution.py:45
  486.5 24.1 %all-to-all-done.14 = bf16[64,3,2048]{2,1,0:T(4,128)(2,1)} async-done(((bf16[64,3,2048]{2,1,0:T(4,128)(2,1)}), bf16[64,3,2048]{2,1,0:T(4,128)(2,1)}, u32[]{:S(2)}, u32[]{:S(2)}) %all-to-all-start.14) | async-done | bytes 786464 | tf_op jit(solution)/shard_map/all_to_all | solution.py:52
  542.1 22.4 %all-to-all-done.16 = bf16[64,3,2048]{2,1,0:T(4,128)(2,1)} async-done(((bf16[64,3,2048]{2,1,0:T(4,128)(2,1)}), bf16[64,3,2048]{2,1,0:T(4,128)(2,1)}, u32[]{:S(2)}, u32[]{:S(2)}) %all-to-all-start.16) | async-done | bytes 786464 | tf_op jit(solution)/shard_map/all_to_all | solution.py:45
  569.6 9.2 all-to-all-start.17
  580.6 26.7 %all-to-all-done.17 = bf16[64,3,2048]{2,1,0:T(4,128)(2,1)} async-done(((bf16[64,3,2048]{2,1,0:T(4,128)(2,1)}), bf16[64,3,2048]{2,1,0:T(4,128)(2,1)}, u32[]{:S(2)}, u32[]{:S(2)}) %all-to-all-start.17) | async-done | bytes 786464 | tf_op jit(solution)/shard_map/all_to_all | solution.py:52
  642.5 23.4 %all-to-all-done.19 = bf16[64,3,2048]{2,1,0:T(4,128)(2,1)} async-done(((bf16[64,3,2048]{2,1,0:T(4,128)(2,1)}), bf16[64,3,2048]{2,1,0:T(4,128)(2,1)}, u32[]{:S(2)}, u32[]{:S(2)}) %all-to-all-start.19) | async-done | bytes 786464 | tf_op jit(solution)/shard_map/all_to_all | solution.py:45
  701.7 20.6 %all-to-all-done.22 = bf16[64,3,2048]{2,1,0:T(4,128)(2,1)} async-done(((bf16[64,3,2048]{2,1,0:T(4,128)(2,1)}), bf16[64,3,2048]{2,1,0:T(4,128)(2,1)}, u32[]{:S(2)}, u32[]{:S(2)}) %all-to-all-start.22) | async-done | bytes 786464 | tf_op jit(solution)/shard_map/all_to_all | solution.py:60
  728.1 14.4 collective-permute-done.6
  750.4 28.5 %all-to-all-done.23 = bf16[64,3,2048]{2,1,0:T(4,128)(2,1)} async-done(((bf16[64,3,2048]{2,1,0:T(4,128)(2,1)}), bf16[64,3,2048]{2,1,0:T(4,128)(2,1)}, u32[]{:S(2)}, u32[]{:S(2)}) %all-to-all-start.23) | async-done | bytes 786464 | tf_op jit(solution)/shard_map/all_to_all | solution.py:56
  788.4 19.0 %all-to-all-done.24 = bf16[64,3,2048]{2,1,0:T(4,128)(2,1)} async-done(((bf16[64,3,2048]{2,1,0:T(4,128)(2,1)}), bf16[64,3,2048]{2,1,0:T(4,128)(2,1)}, u32[]{:S(2)}, u32[]{:S(2)}) %all-to-all-start.24) | async-done | bytes 786464 | tf_op jit(solution)/shard_map/all_to_all | solution.py:60
  812.8 11.5 collective-permute-done.7
  827.4 12.2 all-to-all-start.25
  839.6 28.5 %all-to-all-done.25 = bf16[64,3,2048]{2,1,0:T(4,128)(2,1)} async-done(((bf16[64,3,2048]{2,1,0:T(4,128)(2,1)}), bf16[64,3,2048]{2,1,0:T(4,128)(2,1)}, u32[]{:S(2)}, u32[]{:S(2)}) %all-to-all-start.25) | async-done | bytes 786464 | tf_op jit(solution)/shard_map/all_to_all | solution.py:56
  877.8 19.0 %all-to-all-done.26 = bf16[64,3,2048]{2,1,0:T(4,128)(2,1)} async-done(((bf16[64,3,2048]{2,1,0:T(4,128)(2,1)}), bf16[64,3,2048]{2,1,0:T(4,128)(2,1)}, u32[]{:S(2)}, u32[]{:S(2)}) %all-to-all-start.26) | async-done | bytes 786464 | tf_op jit(solution)/shard_map/all_to_all | solution.py:60
  902.2 17.1 %collective-permute-done.8 = bf16[32,2048]{1,0:T(8,128)(2,1)S(1)} collective-permute-done((bf16[32,2048]{1,0:T(8,128)(2,1)S(1)}, bf16[32,2048]{1,0:T(8,128)(2,1)S(1)}, u32[]{:S(2)}, u32[]{:S(2)}) %collective-permute-start.8) | collective-permute-done | bytes 131104 | tf_op jit(solution)/shard_map/ppermute | solution.py:13
  930.2 28.5 %all-to-all-done.27 = bf16[64,3,2048]{2,1,0:T(4,128)(2,1)} async-done(((bf16[64,3,2048]{2,1,0:T(4,128)(2,1)}), bf16[64,3,2048]{2,1,0:T(4,128)(2,1)}, u32[]{:S(2)}, u32[]{:S(2)}) %all-to-all-start.27) | async-done | bytes 786464 | tf_op jit(solution)/shard_map/all_to_all | solution.py:56
  958.6 9.7 conditional.24
  976.9 19.1 %all-to-all-done.28 = bf16[64,3,2048]{2,1,0:T(4,128)(2,1)} async-done(((bf16[64,3,2048]{2,1,0:T(4,128)(2,1)}), bf16[64,3,2048]{2,1,0:T(4,128)(2,1)}, u32[]{:S(2)}, u32[]{:S(2)}) %all-to-all-start.28) | async-done | bytes 786464 | tf_op jit(solution)/shard_map/all_to_all | solution.py:60
  1020.2 28.5 %all-to-all-done.29 = bf16[64,3,2048]{2,1,0:T(4,128)(2,1)} async-done(((bf16[64,3,2048]{2,1,0:T(4,128)(2,1)}), bf16[64,3,2048]{2,1,0:T(4,128)(2,1)}, u32[]{:S(2)}, u32[]{:S(2)}) %all-to-all-start.29) | async-done | bytes 786464 | tf_op jit(solution)/shard_map/all_to_all | solution.py:56
  1048.7 9.7 conditional.25
  1066.9 19.1 %all-to-all-done.30 = bf16[64,3,2048]{2,1,0:T(4,128)(2,1)} async-done(((bf16[64,3,2048]{2,1,0:T(4,128)(2,1)}), bf16[64,3,2048]{2,1,0:T(4,128)(2,1)}, u32[]{:S(2)}, u32[]{:S(2)}) %all-to-all-start.30) | async-done | bytes 786464 | tf_op jit(solution)/shard_map/all_to_all | solution.py:60
  1091.4 23.4 %collective-permute-done.10 = bf16[32,2048]{1,0:T(8,128)(2,1)S(1)} collective-permute-done((bf16[32,2048]{1,0:T(8,128)(2,1)S(1)}, bf16[32,2048]{1,0:T(8,128)(2,1)S(1)}, u32[]{:S(2)}, u32[]{:S(2)}) %collective-permute-start.10) | collective-permute-done | bytes 131104 | tf_op jit(solution)/shard_map/ppermute | solution.py:13
  1123.6 28.0 %all-to-all-done.31 = bf16[64,3,2048]{2,1,0:T(4,128)(2,1)} async-done(((bf16[64,3,2048]{2,1,0:T(4,128)(2,1)}), bf16[64,3,2048]{2,1,0:T(4,128)(2,1)}, u32[]{:S(2)}, u32[]{:S(2)}) %all-to-all-start.31) | async-done | bytes 786464 | tf_op jit(solution)/shard_map/all_to_all | solution.py:56
  1151.6 9.7 conditional.26
  1170.2 27.8 %all-to-all-done.32 = bf16[64,3,2048]{2,1,0:T(4,128)(2,1)} async-done(((bf16[64,3,2048]{2,1,0:T(4,128)(2,1)}), bf16[64,3,2048]{2,1,0:T(4,128)(2,1)}, u32[]{:S(2)}, u32[]{:S(2)}) %all-to-all-start.32) | async-done | bytes 786464 | tf_op jit(solution)/shard_map/all_to_all | solution.py:60
  1211.5 10.1 all-to-all-start.33
  1224.8 18.5 %all-to-all-done.33 = bf16[64,3,2048]{2,1,0:T(4,128)(2,1)} async-done(((bf16[64,3,2048]{2,1,0:T(4,128)(2,1)}), bf16[64,3,2048]{2,1,0:T(4,128)(2,1)}, u32[]{:S(2)}, u32[]{:S(2)}) %all-to-all-start.33) | async-done | bytes 786464 | tf_op jit(solution)/shard_map/all_to_all | solution.py:56
  1251.3 9.8 conditional.27
  1281.5 18.8 %all-to-all-done.34 = bf16[64,3,2048]{2,1,0:T(4,128)(2,1)S(1)} async-done(((bf16[64,3,2048]{2,1,0:T(4,128)(2,1)}), bf16[64,3,2048]{2,1,0:T(4,128)(2,1)S(1)}, u32[]{:S(2)}, u32[]{:S(2)}) %all-to-all-start.34) | async-done | bytes 786464 | tf_op jit(solution)/shard_map/all_to_all | solution.py:60
  1302.3 203.1 %psum.7 = f32[1,2048]{1,0:T(1,128)} all-reduce(f32[1,2048]{1,0:T(1,128)S(1)} %bitcast.633), channel_id=1, replica_groups=mesh['dp'=8,'pipe'=4,'expert'=8] {'dp','expert'}, use_global_device_ids=true, to_apply=%region_84.85 | all-reduce | flops 2048 | bytes 16384 | tf_op jit(solution)/shard_map/psum | solution.py:226
  (392 shorter events, 527.2 us)
Async XLA Ops:
  5.5 27.2 %all-to-all-start = ((bf16[64,3,1]{1,2,0:T(2,128)(2,1)}), bf16[64,3,1]{1,2,0:T(2,128)(2,1)S(1)}, u32[]{:S(2)}, u32[]{:S(2)}) async-start(bf16[64,3,1]{1,2,0:T(2,128)(2,1)} %copy.214), calls=%async_computation | async-start | bytes 65536 | tf_op jit(solution)/shard_map/all_to_all | solution.py:46
  32.7 33.2 %all-to-all-start.1 = ((bf16[64,3,2048]{2,1,0:T(4,128)(2,1)}), bf16[64,3,2048]{2,1,0:T(4,128)(2,1)}, u32[]{:S(2)}, u32[]{:S(2)}) async-start(bf16[64,3,2048]{2,1,0:T(4,128)(2,1)} %copy.215), calls=%async_computation.1 | async-start | bytes 2097152 | tf_op jit(solution)/shard_map/all_to_all | solution.py:45
  78.3 24.5 %all-to-all-start.2 = ((bf16[64,3,2048]{2,1,0:T(4,128)(2,1)}), bf16[64,3,2048]{2,1,0:T(4,128)(2,1)}, u32[]{:S(2)}, u32[]{:S(2)}) async-start(bf16[64,3,2048]{2,1,0:T(4,128)(2,1)} %reshape.639), calls=%async_computation.2 | async-start | bytes 2097152 | tf_op jit(solution)/shard_map/all_to_all | solution.py:52
  102.8 19.6 %all-to-all-start.3 = ((bf16[64,3,1]{1,2,0:T(2,128)(2,1)}), bf16[64,3,1]{1,2,0:T(2,128)(2,1)S(1)}, u32[]{:S(2)}, u32[]{:S(2)}) async-start(bf16[64,3,1]{1,2,0:T(2,128)(2,1)} %copy.218), calls=%async_computation.3 | async-start | bytes 65536 | tf_op jit(solution)/shard_map/all_to_all | solution.py:46
  109.9 9.6 collective-permute-start
  122.4 43.0 %all-to-all-start.4 = ((bf16[64,3,2048]{2,1,0:T(4,128)(2,1)}), bf16[64,3,2048]{2,1,0:T(4,128)(2,1)}, u32[]{:S(2)}, u32[]{:S(2)}) async-start(bf16[64,3,2048]{2,1,0:T(4,128)(2,1)} %copy.219), calls=%async_computation.4 | async-start | bytes 2097152 | tf_op jit(solution)/shard_map/all_to_all | solution.py:45
  178.0 24.5 %all-to-all-start.5 = ((bf16[64,3,2048]{2,1,0:T(4,128)(2,1)}), bf16[64,3,2048]{2,1,0:T(4,128)(2,1)}, u32[]{:S(2)}, u32[]{:S(2)}) async-start(bf16[64,3,2048]{2,1,0:T(4,128)(2,1)} %reshape.641), calls=%async_computation.5 | async-start | bytes 2097152 | tf_op jit(solution)/shard_map/all_to_all | solution.py:52
  205.4 23.7 %collective-permute-start.1 = (bf16[32,2048]{1,0:T(8,128)(2,1)S(1)}, bf16[32,2048]{1,0:T(8,128)(2,1)S(1)}, u32[]{:S(2)}, u32[]{:S(2)}) collective-permute-start(bf16[32,2048]{1,0:T(8,128)(2,1)S(1)} %get-tuple-element.841), channel_id=1, source_target_pairs={{0,8},{8,16},{16,24},{1,9},{9,17},{17,25},{2,10},{10,18},{18,26},{... | collective-permute-start | bytes 393224 | tf_op jit(solution)/shard_map/ppermute | solution.py:13
  224.3 16.5 %all-to-all-start.6 = ((bf16[64,3,1]{1,2,0:T(2,128)(2,1)}), bf16[64,3,1]{1,2,0:T(2,128)(2,1)S(1)}, u32[]{:S(2)}, u32[]{:S(2)}) async-start(bf16[64,3,1]{1,2,0:T(2,128)(2,1)} %copy.222), calls=%async_computation.6 | async-start | bytes 65536 | tf_op jit(solution)/shard_map/all_to_all | solution.py:46
  240.8 34.5 %all-to-all-start.7 = ((bf16[64,3,2048]{2,1,0:T(4,128)(2,1)}), bf16[64,3,2048]{2,1,0:T(4,128)(2,1)}, u32[]{:S(2)}, u32[]{:S(2)}) async-start(bf16[64,3,2048]{2,1,0:T(4,128)(2,1)} %copy.223), calls=%async_computation.7 | async-start | bytes 2097152 | tf_op jit(solution)/shard_map/all_to_all | solution.py:45
  287.7 31.1 %all-to-all-start.8 = ((bf16[64,3,2048]{2,1,0:T(4,128)(2,1)}), bf16[64,3,2048]{2,1,0:T(4,128)(2,1)}, u32[]{:S(2)}, u32[]{:S(2)}) async-start(bf16[64,3,2048]{2,1,0:T(4,128)(2,1)} %reshape.643), calls=%async_computation.8 | async-start | bytes 2097152 | tf_op jit(solution)/shard_map/all_to_all | solution.py:52
  321.7 11.8 collective-permute-start.2
  324.2 20.9 %all-to-all-start.9 = ((bf16[64,3,1]{1,2,0:T(2,128)(2,1)}), bf16[64,3,1]{1,2,0:T(2,128)(2,1)S(1)}, u32[]{:S(2)}, u32[]{:S(2)}) async-start(bf16[64,3,1]{1,2,0:T(2,128)(2,1)} %copy.226), calls=%async_computation.9 | async-start | bytes 65536 | tf_op jit(solution)/shard_map/all_to_all | solution.py:46
  345.1 32.7 %all-to-all-start.10 = ((bf16[64,3,2048]{2,1,0:T(4,128)(2,1)}), bf16[64,3,2048]{2,1,0:T(4,128)(2,1)}, u32[]{:S(2)}, u32[]{:S(2)}) async-start(bf16[64,3,2048]{2,1,0:T(4,128)(2,1)} %copy.227), calls=%async_computation.10 | async-start | bytes 2097152 | tf_op jit(solution)/shard_map/all_to_all | solution.py:45
  390.2 31.1 %all-to-all-start.11 = ((bf16[64,3,2048]{2,1,0:T(4,128)(2,1)}), bf16[64,3,2048]{2,1,0:T(4,128)(2,1)}, u32[]{:S(2)}, u32[]{:S(2)}) async-start(bf16[64,3,2048]{2,1,0:T(4,128)(2,1)} %reshape.645), calls=%async_computation.11 | async-start | bytes 2097152 | tf_op jit(solution)/shard_map/all_to_all | solution.py:52
  424.2 11.2 collective-permute-start.3
  426.2 20.7 %all-to-all-start.12 = ((bf16[64,3,1]{1,2,0:T(2,128)(2,1)}), bf16[64,3,1]{1,2,0:T(2,128)(2,1)S(1)}, u32[]{:S(2)}, u32[]{:S(2)}) async-start(bf16[64,3,1]{1,2,0:T(2,128)(2,1)} %copy.230), calls=%async_computation.12 | async-start | bytes 65536 | tf_op jit(solution)/shard_map/all_to_all | solution.py:46
  447.0 27.6 %all-to-all-start.13 = ((bf16[64,3,2048]{2,1,0:T(4,128)(2,1)}), bf16[64,3,2048]{2,1,0:T(4,128)(2,1)}, u32[]{:S(2)}, u32[]{:S(2)}) async-start(bf16[64,3,2048]{2,1,0:T(4,128)(2,1)} %copy.231), calls=%async_computation.13 | async-start | bytes 2097152 | tf_op jit(solution)/shard_map/all_to_all | solution.py:45
  479.9 30.7 %all-to-all-start.14 = ((bf16[64,3,2048]{2,1,0:T(4,128)(2,1)}), bf16[64,3,2048]{2,1,0:T(4,128)(2,1)}, u32[]{:S(2)}, u32[]{:S(2)}) async-start(bf16[64,3,2048]{2,1,0:T(4,128)(2,1)} %reshape.647), calls=%async_computation.14 | async-start | bytes 2097152 | tf_op jit(solution)/shard_map/all_to_all | solution.py:52
  513.5 11.1 collective-permute-start.4
  517.5 18.8 %all-to-all-start.15 = ((bf16[64,3,1]{1,2,0:T(2,128)(2,1)}), bf16[64,3,1]{1,2,0:T(2,128)(2,1)S(1)}, u32[]{:S(2)}, u32[]{:S(2)}) async-start(bf16[64,3,1]{1,2,0:T(2,128)(2,1)} %copy.234), calls=%async_computation.15 | async-start | bytes 65536 | tf_op jit(solution)/shard_map/all_to_all | solution.py:46
  536.3 28.2 %all-to-all-start.16 = ((bf16[64,3,2048]{2,1,0:T(4,128)(2,1)}), bf16[64,3,2048]{2,1,0:T(4,128)(2,1)}, u32[]{:S(2)}, u32[]{:S(2)}) async-start(bf16[64,3,2048]{2,1,0:T(4,128)(2,1)} %copy.235), calls=%async_computation.16 | async-start | bytes 2097152 | tf_op jit(solution)/shard_map/all_to_all | solution.py:45
  569.6 37.7 %all-to-all-start.17 = ((bf16[64,3,2048]{2,1,0:T(4,128)(2,1)}), bf16[64,3,2048]{2,1,0:T(4,128)(2,1)}, u32[]{:S(2)}, u32[]{:S(2)}) async-start(bf16[64,3,2048]{2,1,0:T(4,128)(2,1)} %reshape.649), calls=%async_computation.17 | async-start | bytes 2097152 | tf_op jit(solution)/shard_map/all_to_all | solution.py:52
  610.2 9.8 collective-permute-start.5
  612.5 19.1 %all-to-all-start.18 = ((bf16[64,3,1]{1,2,0:T(2,128)(2,1)}), bf16[64,3,1]{1,2,0:T(2,128)(2,1)S(1)}, u32[]{:S(2)}, u32[]{:S(2)}) async-start(bf16[64,3,1]{1,2,0:T(2,128)(2,1)} %copy.238), calls=%async_computation.18 | async-start | bytes 65536 | tf_op jit(solution)/shard_map/all_to_all | solution.py:46
  631.6 34.4 %all-to-all-start.19 = ((bf16[64,3,2048]{2,1,0:T(4,128)(2,1)}), bf16[64,3,2048]{2,1,0:T(4,128)(2,1)}, u32[]{:S(2)}, u32[]{:S(2)}) async-start(bf16[64,3,2048]{2,1,0:T(4,128)(2,1)} %copy.239), calls=%async_computation.19 | async-start | bytes 2097152 | tf_op jit(solution)/shard_map/all_to_all | solution.py:45
  666.0 24.4 %all-to-all-start.21 = ((bf16[64,3,2048]{2,1,0:T(4,128)(2,1)}), bf16[64,3,2048]{2,1,0:T(4,128)(2,1)}, u32[]{:S(2)}, u32[]{:S(2)}) async-start(bf16[64,3,2048]{2,1,0:T(4,128)(2,1)} %copy.242), calls=%async_computation.21 | async-start | bytes 2097152 | tf_op jit(solution)/shard_map/all_to_all | solution.py:56
  694.6 27.6 %all-to-all-start.22 = ((bf16[64,3,2048]{2,1,0:T(4,128)(2,1)}), bf16[64,3,2048]{2,1,0:T(4,128)(2,1)}, u32[]{:S(2)}, u32[]{:S(2)}) async-start(bf16[64,3,2048]{2,1,0:T(4,128)(2,1)} %reshape.654), calls=%async_computation.22 | async-start | bytes 2097152 | tf_op jit(solution)/shard_map/all_to_all | solution.py:60
  726.8 15.7 %collective-permute-start.6 = (bf16[32,2048]{1,0:T(8,128)(2,1)S(1)}, bf16[32,2048]{1,0:T(8,128)(2,1)S(1)}, u32[]{:S(2)}, u32[]{:S(2)}) collective-permute-start(bf16[32,2048]{1,0:T(8,128)(2,1)S(1)} %get-tuple-element.790), channel_id=1, source_target_pairs={{8,0},{16,8},{24,16},{9,1},{17,9},{25,17},{10,2},{18,10},{26,18},{... | collective-permute-start | bytes 393224 | tf_op jit(solution)/shard_map/ppermute | solution.py:13
  744.6 34.2 %all-to-all-start.23 = ((bf16[64,3,2048]{2,1,0:T(4,128)(2,1)}), bf16[64,3,2048]{2,1,0:T(4,128)(2,1)}, u32[]{:S(2)}, u32[]{:S(2)}) async-start(bf16[64,3,2048]{2,1,0:T(4,128)(2,1)} %copy.251), calls=%async_computation.23 | async-start | bytes 2097152 | tf_op jit(solution)/shard_map/all_to_all | solution.py:56
  783.1 24.3 %all-to-all-start.24 = ((bf16[64,3,2048]{2,1,0:T(4,128)(2,1)}), bf16[64,3,2048]{2,1,0:T(4,128)(2,1)}, u32[]{:S(2)}, u32[]{:S(2)}) async-start(bf16[64,3,2048]{2,1,0:T(4,128)(2,1)} %reshape.656), calls=%async_computation.24 | async-start | bytes 2097152 | tf_op jit(solution)/shard_map/all_to_all | solution.py:60
  811.5 12.8 collective-permute-start.7
  827.4 40.7 %all-to-all-start.25 = ((bf16[64,3,2048]{2,1,0:T(4,128)(2,1)}), bf16[64,3,2048]{2,1,0:T(4,128)(2,1)}, u32[]{:S(2)}, u32[]{:S(2)}) async-start(bf16[64,3,2048]{2,1,0:T(4,128)(2,1)} %copy.253), calls=%async_computation.25 | async-start | bytes 2097152 | tf_op jit(solution)/shard_map/all_to_all | solution.py:56
  872.5 24.3 %all-to-all-start.26 = ((bf16[64,3,2048]{2,1,0:T(4,128)(2,1)}), bf16[64,3,2048]{2,1,0:T(4,128)(2,1)}, u32[]{:S(2)}, u32[]{:S(2)}) async-start(bf16[64,3,2048]{2,1,0:T(4,128)(2,1)} %reshape.658), calls=%async_computation.26 | async-start | bytes 2097152 | tf_op jit(solution)/shard_map/all_to_all | solution.py:60
  900.9 18.4 %collective-permute-start.8 = (bf16[32,2048]{1,0:T(8,128)(2,1)S(1)}, bf16[32,2048]{1,0:T(8,128)(2,1)S(1)}, u32[]{:S(2)}, u32[]{:S(2)}) collective-permute-start(bf16[32,2048]{1,0:T(8,128)(2,1)S(1)} %get-tuple-element.786), channel_id=1, source_target_pairs={{8,0},{16,8},{24,16},{9,1},{17,9},{25,17},{10,2},{18,10},{26,18},{... | collective-permute-start | bytes 393224 | tf_op jit(solution)/shard_map/ppermute | solution.py:13
  922.4 36.3 %all-to-all-start.27 = ((bf16[64,3,2048]{2,1,0:T(4,128)(2,1)}), bf16[64,3,2048]{2,1,0:T(4,128)(2,1)}, u32[]{:S(2)}, u32[]{:S(2)}) async-start(bf16[64,3,2048]{2,1,0:T(4,128)(2,1)} %copy.255), calls=%async_computation.27 | async-start | bytes 2097152 | tf_op jit(solution)/shard_map/all_to_all | solution.py:56
  971.6 24.4 %all-to-all-start.28 = ((bf16[64,3,2048]{2,1,0:T(4,128)(2,1)}), bf16[64,3,2048]{2,1,0:T(4,128)(2,1)}, u32[]{:S(2)}, u32[]{:S(2)}) async-start(bf16[64,3,2048]{2,1,0:T(4,128)(2,1)} %reshape.660), calls=%async_computation.28 | async-start | bytes 2097152 | tf_op jit(solution)/shard_map/all_to_all | solution.py:60
  1000.1 9.3 collective-permute-start.9
  1012.4 36.3 %all-to-all-start.29 = ((bf16[64,3,2048]{2,1,0:T(4,128)(2,1)}), bf16[64,3,2048]{2,1,0:T(4,128)(2,1)}, u32[]{:S(2)}, u32[]{:S(2)}) async-start(bf16[64,3,2048]{2,1,0:T(4,128)(2,1)} %copy.257), calls=%async_computation.29 | async-start | bytes 2097152 | tf_op jit(solution)/shard_map/all_to_all | solution.py:56
  1061.6 24.4 %all-to-all-start.30 = ((bf16[64,3,2048]{2,1,0:T(4,128)(2,1)}), bf16[64,3,2048]{2,1,0:T(4,128)(2,1)}, u32[]{:S(2)}, u32[]{:S(2)}) async-start(bf16[64,3,2048]{2,1,0:T(4,128)(2,1)} %reshape.662), calls=%async_computation.30 | async-start | bytes 2097152 | tf_op jit(solution)/shard_map/all_to_all | solution.py:60
  1090.1 24.7 %collective-permute-start.10 = (bf16[32,2048]{1,0:T(8,128)(2,1)S(1)}, bf16[32,2048]{1,0:T(8,128)(2,1)S(1)}, u32[]{:S(2)}, u32[]{:S(2)}) collective-permute-start(bf16[32,2048]{1,0:T(8,128)(2,1)S(1)} %get-tuple-element.782), channel_id=1, source_target_pairs={{8,0},{16,8},{24,16},{9,1},{17,9},{25,17},{10,2},{18,10},{26,18},{... | collective-permute-start | bytes 393224 | tf_op jit(solution)/shard_map/ppermute | solution.py:13
  1117.9 33.7 %all-to-all-start.31 = ((bf16[64,3,2048]{2,1,0:T(4,128)(2,1)}), bf16[64,3,2048]{2,1,0:T(4,128)(2,1)}, u32[]{:S(2)}, u32[]{:S(2)}) async-start(bf16[64,3,2048]{2,1,0:T(4,128)(2,1)} %copy.259), calls=%async_computation.31 | async-start | bytes 2097152 | tf_op jit(solution)/shard_map/all_to_all | solution.py:56
  1164.6 33.5 %all-to-all-start.32 = ((bf16[64,3,2048]{2,1,0:T(4,128)(2,1)}), bf16[64,3,2048]{2,1,0:T(4,128)(2,1)}, u32[]{:S(2)}, u32[]{:S(2)}) async-start(bf16[64,3,2048]{2,1,0:T(4,128)(2,1)} %reshape.664), calls=%async_computation.32 | async-start | bytes 2097152 | tf_op jit(solution)/shard_map/all_to_all | solution.py:60
  1202.1 6.4 collective-permute-start.11
  1211.5 31.9 %all-to-all-start.33 = ((bf16[64,3,2048]{2,1,0:T(4,128)(2,1)}), bf16[64,3,2048]{2,1,0:T(4,128)(2,1)}, u32[]{:S(2)}, u32[]{:S(2)}) async-start(bf16[64,3,2048]{2,1,0:T(4,128)(2,1)} %copy.261), calls=%async_computation.33 | async-start | bytes 2097152 | tf_op jit(solution)/shard_map/all_to_all | solution.py:56
  1243.3 29.7 %all-to-all-start.20 = ((bf16[64,3,2048]{2,1,0:T(4,128)(2,1)}), bf16[64,3,2048]{2,1,0:T(4,128)(2,1)}, u32[]{:S(2)}, u32[]{:S(2)}) async-start(bf16[64,3,2048]{2,1,0:T(4,128)(2,1)} %reshape.651), calls=%async_computation.20 | async-start | bytes 2097152 | tf_op jit(solution)/shard_map/all_to_all | solution.py:52
  1273.1 27.2 %all-to-all-start.34 = ((bf16[64,3,2048]{2,1,0:T(4,128)(2,1)}), bf16[64,3,2048]{2,1,0:T(4,128)(2,1)S(1)}, u32[]{:S(2)}, u32[]{:S(2)}) async-start(bf16[64,3,2048]{2,1,0:T(4,128)(2,1)} %reshape.666), calls=%async_computation.34 | async-start | bytes 2097152 | tf_op jit(solution)/shard_map/all_to_all | solution.py:60
  1278.3 227.0 %copy-start.4 = (bf16[5,32,2048]{2,1,0:T(8,128)(2,1)S(1)}, bf16[5,32,2048]{2,1,0:T(8,128)(2,1)}, u32[]{:S(2)}) copy-start(bf16[5,32,2048]{2,1,0:T(8,128)(2,1)} %get-tuple-element.779) | copy-start | bytes 1966084
  (27 other events, 207.4 us)
where the time goes:
time: 1520 us; the launch traced here: 1510 us
  waiting for transfers between devices  747 us (49%)
  starting transfers between devices  290 us (19%)
  blocking collectives  203 us (13%)
  local copies, waits for them, and re-layouts  141 us (9%)
  matrix products  92.5 us (6%)
  other arithmetic  31.6 us (2%)
    psum x1, blocking collectives, body(): gain_grad = lax.psum(gain_sum, ('dp', 'expert'))  203 us
    all_to_all x7, waiting for transfers between devices, send_rows(): lax.all_to_all(row_block, ('dp', 'expert'), split_axis=0, concat_axis=0,...  177 us
    all_to_all x7, waiting for transfers between devices, send_grads(): lax.all_to_all(row_block, ('dp', 'expert'), split_axis=0, concat_axis=0,...  165 us
    all_to_all x7, waiting for transfers between devices, return_grads(): lax.all_to_all(row_block, ('dp', 'expert'), split_axis=0, concat_axis=0,...  144 us
    all_to_all x7, waiting for transfers between devices, return_rows(): lax.all_to_all(row_block, ('dp', 'expert'), split_axis=0, concat_axis=0,...  138 us
    ppermute x12, waiting for transfers between devices, from_behind(): lax.ppermute(value, axis, [(source, source + steps) for source in range(l...  79.9 us
    all_to_all x7, starting transfers between devices, send_rows(): lax.all_to_all(pair_block, ('dp', 'expert'), split_axis=0, concat_axis=0,...  58 us
    all_to_all x7, starting transfers between devices, send_grads(): lax.all_to_all(row_block, ('dp', 'expert'), split_axis=0, concat_axis=0,...  54.3 us
  transfers between devices with their start and end apart: 47, of which 41 were waited for; matrix products, arithmetic and copies ran while one was open for 5% of the time, Pallas kernels for 0%

commit v1 on v0

--- a/solution.py
+++ b/solution.py
@@ -223,7 +223,9 @@
         gain_sum = gain_sum + gain_term
         if tick_num + 1 < ticks:
             incoming = from_behind(grad_bf, "pipe", -1)
-    gain_grad = lax.psum(gain_sum, ("dp", "expert"))
+    gain_grad = gain_sum
+    for p in ("dp", "expert"):
+        gain_grad = lax.psum(gain_grad, p)
     segment_out = layer_outs[:MICRO].reshape(1, tok_rows, width)
     segment_grad = grad_outs[:MICRO].reshape(1, tok_rows, width)
     return (segment_out, segment_grad, gain_grad.reshape(1, width))

time: 1520 us -> 1360 us (0.89)
  blocking collectives: 203 us -> 38.5 us
    psum x1 -> x2, blocking collectives: 203 us -> 38.5 us  [body(): gain_grad = lax.psum(gain_grad, p)]
  transfers between devices with their start and end apart: 47 -> 47, of which waited for: 41 -> 41; matrix products, arithmetic and copies ran while one was open for 5% -> 6% of each run, Pallas kernels for 0% -> 0%
where the time goes in v1:
time: 1360 us; the launch traced here: 1340 us
  waiting for transfers between devices  747 us (55%)
  starting transfers between devices  290 us (21%)
  local copies, waits for them, and re-layouts  141 us (10%)
  matrix products  92.5 us (7%)
  blocking collectives  38.5 us (3%)
  other arithmetic  31.6 us (2%)
    all_to_all x7, waiting for transfers between devices, send_rows(): lax.all_to_all(row_block, ('dp', 'expert'), split_axis=0, concat_axis=0,...  177 us
    all_to_all x7, waiting for transfers between devices, send_grads(): lax.all_to_all(row_block, ('dp', 'expert'), split_axis=0, concat_axis=0,...  165 us
    all_to_all x7, waiting for transfers between devices, return_grads(): lax.all_to_all(row_block, ('dp', 'expert'), split_axis=0, concat_axis=0,...  144 us
    all_to_all x7, waiting for transfers between devices, return_rows(): lax.all_to_all(row_block, ('dp', 'expert'), split_axis=0, concat_axis=0,...  138 us
    ppermute x12, waiting for transfers between devices, from_behind(): lax.ppermute(value, axis, [(source, source + steps) for source in range(l...  79.9 us
    all_to_all x7, starting transfers between devices, send_rows(): lax.all_to_all(pair_block, ('dp', 'expert'), split_axis=0, concat_axis=0,...  58 us
    all_to_all x7, starting transfers between devices, send_grads(): lax.all_to_all(row_block, ('dp', 'expert'), split_axis=0, concat_axis=0,...  54.3 us
    all_to_all x7, starting transfers between devices, return_rows(): lax.all_to_all(row_block, ('dp', 'expert'), split_axis=0, concat_axis=0,...  50.9 us
  transfers between devices with their start and end apart: 47, of which 41 were waited for; matrix products, arithmetic and copies ran while one was open for 6% of the time, Pallas kernels for 0%

profile of v1, /device:TPU:1, one launch (start us, length us, event | category | flops | bytes accessed | tf_op | source)
XLA Modules:
  0.0 1343.2 jit_solution(13355156007193338560)
XLA Ops:
  5.5 15.6 %all-to-all-start = ((bf16[64,3,1]{1,2,0:T(2,128)(2,1)}), bf16[64,3,1]{1,2,0:T(2,128)(2,1)S(1)}, u32[]{:S(2)}, u32[]{:S(2)}) async-start(bf16[64,3,1]{1,2,0:T(2,128)(2,1)} %copy.214), calls=%async_computation | async-start | bytes 65536 | tf_op jit(solution)/shard_map/all_to_all | solution.py:46
  40.4 25.5 %all-to-all-done.1 = bf16[64,3,2048]{2,1,0:T(4,128)(2,1)} async-done(((bf16[64,3,2048]{2,1,0:T(4,128)(2,1)}), bf16[64,3,2048]{2,1,0:T(4,128)(2,1)}, u32[]{:S(2)}, u32[]{:S(2)}) %all-to-all-start.1) | async-done | bytes 786464 | tf_op jit(solution)/shard_map/all_to_all | solution.py:45
  65.9 9.1 conditional.14
  84.8 18.1 %all-to-all-done.2 = bf16[64,3,2048]{2,1,0:T(4,128)(2,1)} async-done(((bf16[64,3,2048]{2,1,0:T(4,128)(2,1)}), bf16[64,3,2048]{2,1,0:T(4,128)(2,1)}, u32[]{:S(2)}, u32[]{:S(2)}) %all-to-all-start.2) | async-done | bytes 786464 | tf_op jit(solution)/shard_map/all_to_all | solution.py:52
  122.4 14.5 %all-to-all-start.4 = ((bf16[64,3,2048]{2,1,0:T(4,128)(2,1)}), bf16[64,3,2048]{2,1,0:T(4,128)(2,1)}, u32[]{:S(2)}, u32[]{:S(2)}) async-start(bf16[64,3,2048]{2,1,0:T(4,128)(2,1)} %copy.219), calls=%async_computation.4 | async-start | bytes 2097152 | tf_op jit(solution)/shard_map/all_to_all | solution.py:45
  136.9 28.5 %all-to-all-done.4 = bf16[64,3,2048]{2,1,0:T(4,128)(2,1)} async-done(((bf16[64,3,2048]{2,1,0:T(4,128)(2,1)}), bf16[64,3,2048]{2,1,0:T(4,128)(2,1)}, u32[]{:S(2)}, u32[]{:S(2)}) %all-to-all-start.4) | async-done | bytes 786464 | tf_op jit(solution)/shard_map/all_to_all | solution.py:45
  165.4 9.3 conditional.15
  184.1 18.4 %all-to-all-done.5 = bf16[64,3,2048]{2,1,0:T(4,128)(2,1)} async-done(((bf16[64,3,2048]{2,1,0:T(4,128)(2,1)}), bf16[64,3,2048]{2,1,0:T(4,128)(2,1)}, u32[]{:S(2)}, u32[]{:S(2)}) %all-to-all-start.5) | async-done | bytes 786464 | tf_op jit(solution)/shard_map/all_to_all | solution.py:52
  205.4 17.4 %collective-permute-start.1 = (bf16[32,2048]{1,0:T(8,128)(2,1)S(1)}, bf16[32,2048]{1,0:T(8,128)(2,1)S(1)}, u32[]{:S(2)}, u32[]{:S(2)}) collective-permute-start(bf16[32,2048]{1,0:T(8,128)(2,1)S(1)} %get-tuple-element.841), channel_id=1, source_target_pairs={{0,8},{8,16},{16,24},{1,9},{9,17},{17,25},{2,10},{10,18},{18,26},{... | collective-permute-start | bytes 393224 | tf_op jit(solution)/shard_map/ppermute | solution.py:13
  246.7 28.6 %all-to-all-done.7 = bf16[64,3,2048]{2,1,0:T(4,128)(2,1)} async-done(((bf16[64,3,2048]{2,1,0:T(4,128)(2,1)}), bf16[64,3,2048]{2,1,0:T(4,128)(2,1)}, u32[]{:S(2)}, u32[]{:S(2)}) %all-to-all-start.7) | async-done | bytes 786464 | tf_op jit(solution)/shard_map/all_to_all | solution.py:45
  275.3 9.1 conditional.16
  298.6 20.2 %all-to-all-done.8 = bf16[64,3,2048]{2,1,0:T(4,128)(2,1)} async-done(((bf16[64,3,2048]{2,1,0:T(4,128)(2,1)}), bf16[64,3,2048]{2,1,0:T(4,128)(2,1)}, u32[]{:S(2)}, u32[]{:S(2)}) %all-to-all-start.8) | async-done | bytes 786464 | tf_op jit(solution)/shard_map/all_to_all | solution.py:52
  324.2 9.3 all-to-all-start.9
  350.9 26.9 %all-to-all-done.10 = bf16[64,3,2048]{2,1,0:T(4,128)(2,1)} async-done(((bf16[64,3,2048]{2,1,0:T(4,128)(2,1)}), bf16[64,3,2048]{2,1,0:T(4,128)(2,1)}, u32[]{:S(2)}, u32[]{:S(2)}) %all-to-all-start.10) | async-done | bytes 786464 | tf_op jit(solution)/shard_map/all_to_all | solution.py:45
  377.8 9.1 conditional.17
  390.2 9.2 all-to-all-start.11
  399.7 21.5 %all-to-all-done.11 = bf16[64,3,2048]{2,1,0:T(4,128)(2,1)} async-done(((bf16[64,3,2048]{2,1,0:T(4,128)(2,1)}), bf16[64,3,2048]{2,1,0:T(4,128)(2,1)}, u32[]{:S(2)}, u32[]{:S(2)}) %all-to-all-start.11) | async-done | bytes 786464 | tf_op jit(solution)/shard_map/all_to_all | solution.py:52
  452.8 21.8 %all-to-all-done.13 = bf16[64,3,2048]{2,1,0:T(4,128)(2,1)} async-done(((bf16[64,3,2048]{2,1,0:T(4,128)(2,1)}), bf16[64,3,2048]{2,1,0:T(4,128)(2,1)}, u32[]{:S(2)}, u32[]{:S(2)}) %all-to-all-start.13) | async-done | bytes 786464 | tf_op jit(solution)/shard_map/all_to_all | solution.py:45
  486.5 24.1 %all-to-all-done.14 = bf16[64,3,2048]{2,1,0:T(4,128)(2,1)} async-done(((bf16[64,3,2048]{2,1,0:T(4,128)(2,1)}), bf16[64,3,2048]{2,1,0:T(4,128)(2,1)}, u32[]{:S(2)}, u32[]{:S(2)}) %all-to-all-start.14) | async-done | bytes 786464 | tf_op jit(solution)/shard_map/all_to_all | solution.py:52
  542.1 22.4 %all-to-all-done.16 = bf16[64,3,2048]{2,1,0:T(4,128)(2,1)} async-done(((bf16[64,3,2048]{2,1,0:T(4,128)(2,1)}), bf16[64,3,2048]{2,1,0:T(4,128)(2,1)}, u32[]{:S(2)}, u32[]{:S(2)}) %all-to-all-start.16) | async-done | bytes 786464 | tf_op jit(solution)/shard_map/all_to_all | solution.py:45
  569.6 9.2 all-to-all-start.17
  580.6 26.7 %all-to-all-done.17 = bf16[64,3,2048]{2,1,0:T(4,128)(2,1)} async-done(((bf16[64,3,2048]{2,1,0:T(4,128)(2,1)}), bf16[64,3,2048]{2,1,0:T(4,128)(2,1)}, u32[]{:S(2)}, u32[]{:S(2)}) %all-to-all-start.17) | async-done | bytes 786464 | tf_op jit(solution)/shard_map/all_to_all | solution.py:52
  642.5 23.4 %all-to-all-done.19 = bf16[64,3,2048]{2,1,0:T(4,128)(2,1)} async-done(((bf16[64,3,2048]{2,1,0:T(4,128)(2,1)}), bf16[64,3,2048]{2,1,0:T(4,128)(2,1)}, u32[]{:S(2)}, u32[]{:S(2)}) %all-to-all-start.19) | async-done | bytes 786464 | tf_op jit(solution)/shard_map/all_to_all | solution.py:45
  701.7 20.6 %all-to-all-done.22 = bf16[64,3,2048]{2,1,0:T(4,128)(2,1)} async-done(((bf16[64,3,2048]{2,1,0:T(4,128)(2,1)}), bf16[64,3,2048]{2,1,0:T(4,128)(2,1)}, u32[]{:S(2)}, u32[]{:S(2)}) %all-to-all-start.22) | async-done | bytes 786464 | tf_op jit(solution)/shard_map/all_to_all | solution.py:60
  728.1 14.4 %collective-permute-done.6 = bf16[32,2048]{1,0:T(8,128)(2,1)S(1)} collective-permute-done((bf16[32,2048]{1,0:T(8,128)(2,1)S(1)}, bf16[32,2048]{1,0:T(8,128)(2,1)S(1)}, u32[]{:S(2)}, u32[]{:S(2)}) %collective-permute-start.6) | collective-permute-done | bytes 131104 | tf_op jit(solution)/shard_map/ppermute | solution.py:13
  750.4 28.5 %all-to-all-done.23 = bf16[64,3,2048]{2,1,0:T(4,128)(2,1)} async-done(((bf16[64,3,2048]{2,1,0:T(4,128)(2,1)}), bf16[64,3,2048]{2,1,0:T(4,128)(2,1)}, u32[]{:S(2)}, u32[]{:S(2)}) %all-to-all-start.23) | async-done | bytes 786464 | tf_op jit(solution)/shard_map/all_to_all | solution.py:56
  788.4 19.0 %all-to-all-done.24 = bf16[64,3,2048]{2,1,0:T(4,128)(2,1)} async-done(((bf16[64,3,2048]{2,1,0:T(4,128)(2,1)}), bf16[64,3,2048]{2,1,0:T(4,128)(2,1)}, u32[]{:S(2)}, u32[]{:S(2)}) %all-to-all-start.24) | async-done | bytes 786464 | tf_op jit(solution)/shard_map/all_to_all | solution.py:60
  812.8 11.5 collective-permute-done.7
  827.4 12.2 all-to-all-start.25
  839.6 28.5 %all-to-all-done.25 = bf16[64,3,2048]{2,1,0:T(4,128)(2,1)} async-done(((bf16[64,3,2048]{2,1,0:T(4,128)(2,1)}), bf16[64,3,2048]{2,1,0:T(4,128)(2,1)}, u32[]{:S(2)}, u32[]{:S(2)}) %all-to-all-start.25) | async-done | bytes 786464 | tf_op jit(solution)/shard_map/all_to_all | solution.py:56
  877.8 19.0 %all-to-all-done.26 = bf16[64,3,2048]{2,1,0:T(4,128)(2,1)} async-done(((bf16[64,3,2048]{2,1,0:T(4,128)(2,1)}), bf16[64,3,2048]{2,1,0:T(4,128)(2,1)}, u32[]{:S(2)}, u32[]{:S(2)}) %all-to-all-start.26) | async-done | bytes 786464 | tf_op jit(solution)/shard_map/all_to_all | solution.py:60
  902.2 17.1 %collective-permute-done.8 = bf16[32,2048]{1,0:T(8,128)(2,1)S(1)} collective-permute-done((bf16[32,2048]{1,0:T(8,128)(2,1)S(1)}, bf16[32,2048]{1,0:T(8,128)(2,1)S(1)}, u32[]{:S(2)}, u32[]{:S(2)}) %collective-permute-start.8) | collective-permute-done | bytes 131104 | tf_op jit(solution)/shard_map/ppermute | solution.py:13
  930.2 28.5 %all-to-all-done.27 = bf16[64,3,2048]{2,1,0:T(4,128)(2,1)} async-done(((bf16[64,3,2048]{2,1,0:T(4,128)(2,1)}), bf16[64,3,2048]{2,1,0:T(4,128)(2,1)}, u32[]{:S(2)}, u32[]{:S(2)}) %all-to-all-start.27) | async-done | bytes 786464 | tf_op jit(solution)/shard_map/all_to_all | solution.py:56
  958.6 9.7 conditional.24
  976.9 19.1 %all-to-all-done.28 = bf16[64,3,2048]{2,1,0:T(4,128)(2,1)} async-done(((bf16[64,3,2048]{2,1,0:T(4,128)(2,1)}), bf16[64,3,2048]{2,1,0:T(4,128)(2,1)}, u32[]{:S(2)}, u32[]{:S(2)}) %all-to-all-start.28) | async-done | bytes 786464 | tf_op jit(solution)/shard_map/all_to_all | solution.py:60
  1020.2 28.5 %all-to-all-done.29 = bf16[64,3,2048]{2,1,0:T(4,128)(2,1)} async-done(((bf16[64,3,2048]{2,1,0:T(4,128)(2,1)}), bf16[64,3,2048]{2,1,0:T(4,128)(2,1)}, u32[]{:S(2)}, u32[]{:S(2)}) %all-to-all-start.29) | async-done | bytes 786464 | tf_op jit(solution)/shard_map/all_to_all | solution.py:56
  1048.7 9.7 conditional.25
  1066.9 19.1 %all-to-all-done.30 = bf16[64,3,2048]{2,1,0:T(4,128)(2,1)} async-done(((bf16[64,3,2048]{2,1,0:T(4,128)(2,1)}), bf16[64,3,2048]{2,1,0:T(4,128)(2,1)}, u32[]{:S(2)}, u32[]{:S(2)}) %all-to-all-start.30) | async-done | bytes 786464 | tf_op jit(solution)/shard_map/all_to_all | solution.py:60
  1091.4 23.4 %collective-permute-done.10 = bf16[32,2048]{1,0:T(8,128)(2,1)S(1)} collective-permute-done((bf16[32,2048]{1,0:T(8,128)(2,1)S(1)}, bf16[32,2048]{1,0:T(8,128)(2,1)S(1)}, u32[]{:S(2)}, u32[]{:S(2)}) %collective-permute-start.10) | collective-permute-done | bytes 131104 | tf_op jit(solution)/shard_map/ppermute | solution.py:13
  1123.6 28.0 %all-to-all-done.31 = bf16[64,3,2048]{2,1,0:T(4,128)(2,1)} async-done(((bf16[64,3,2048]{2,1,0:T(4,128)(2,1)}), bf16[64,3,2048]{2,1,0:T(4,128)(2,1)}, u32[]{:S(2)}, u32[]{:S(2)}) %all-to-all-start.31) | async-done | bytes 786464 | tf_op jit(solution)/shard_map/all_to_all | solution.py:56
  1151.6 9.7 conditional.26
  1170.2 27.8 %all-to-all-done.32 = bf16[64,3,2048]{2,1,0:T(4,128)(2,1)} async-done(((bf16[64,3,2048]{2,1,0:T(4,128)(2,1)}), bf16[64,3,2048]{2,1,0:T(4,128)(2,1)}, u32[]{:S(2)}, u32[]{:S(2)}) %all-to-all-start.32) | async-done | bytes 786464 | tf_op jit(solution)/shard_map/all_to_all | solution.py:60
  1211.5 10.1 all-to-all-start.33
  1224.8 18.5 %all-to-all-done.33 = bf16[64,3,2048]{2,1,0:T(4,128)(2,1)} async-done(((bf16[64,3,2048]{2,1,0:T(4,128)(2,1)}), bf16[64,3,2048]{2,1,0:T(4,128)(2,1)}, u32[]{:S(2)}, u32[]{:S(2)}) %all-to-all-start.33) | async-done | bytes 786464 | tf_op jit(solution)/shard_map/all_to_all | solution.py:56
  1251.3 9.8 conditional.27
  1281.5 18.8 %all-to-all-done.34 = bf16[64,3,2048]{2,1,0:T(4,128)(2,1)S(1)} async-done(((bf16[64,3,2048]{2,1,0:T(4,128)(2,1)}), bf16[64,3,2048]{2,1,0:T(4,128)(2,1)S(1)}, u32[]{:S(2)}, u32[]{:S(2)}) %all-to-all-start.34) | async-done | bytes 786464 | tf_op jit(solution)/shard_map/all_to_all | solution.py:60
  1302.3 21.5 %psum.14 = f32[2048]{0:T(1024)S(1)} all-reduce(f32[2048]{0:T(1024)S(1)} %select_add_fusion), channel_id=1, replica_groups=mesh['dp'=8,'pipe'=4,'expert'=8] {'dp'}, use_global_device_ids=true, to_apply=%region_84.85 | all-reduce | flops 2048 | bytes 16384 | tf_op jit(solution)/shard_map/psum | solution.py:228
  1323.8 17.0 %psum.15 = f32[1,2048]{1,0:T(1,128)} all-reduce(f32[1,2048]{1,0:T(1,128)S(1)} %bitcast.633), channel_id=1, replica_groups=mesh['dp'=8,'pipe'=4,'expert'=8] {'expert'}, use_global_device_ids=true, to_apply=%region_85.86 | all-reduce | flops 2048 | bytes 16384 | tf_op jit(solution)/shard_map/psum | solution.py:228
  (393 shorter events, 536.2 us)
Async XLA Ops:
  5.5 27.2 %all-to-all-start = ((bf16[64,3,1]{1,2,0:T(2,128)(2,1)}), bf16[64,3,1]{1,2,0:T(2,128)(2,1)S(1)}, u32[]{:S(2)}, u32[]{:S(2)}) async-start(bf16[64,3,1]{1,2,0:T(2,128)(2,1)} %copy.214), calls=%async_computation | async-start | bytes 65536 | tf_op jit(solution)/shard_map/all_to_all | solution.py:46
  32.7 33.2 %all-to-all-start.1 = ((bf16[64,3,2048]{2,1,0:T(4,128)(2,1)}), bf16[64,3,2048]{2,1,0:T(4,128)(2,1)}, u32[]{:S(2)}, u32[]{:S(2)}) async-start(bf16[64,3,2048]{2,1,0:T(4,128)(2,1)} %copy.215), calls=%async_computation.1 | async-start | bytes 2097152 | tf_op jit(solution)/shard_map/all_to_all | solution.py:45
  78.3 24.5 %all-to-all-start.2 = ((bf16[64,3,2048]{2,1,0:T(4,128)(2,1)}), bf16[64,3,2048]{2,1,0:T(4,128)(2,1)}, u32[]{:S(2)}, u32[]{:S(2)}) async-start(bf16[64,3,2048]{2,1,0:T(4,128)(2,1)} %reshape.639), calls=%async_computation.2 | async-start | bytes 2097152 | tf_op jit(solution)/shard_map/all_to_all | solution.py:52
  102.8 19.6 %all-to-all-start.3 = ((bf16[64,3,1]{1,2,0:T(2,128)(2,1)}), bf16[64,3,1]{1,2,0:T(2,128)(2,1)S(1)}, u32[]{:S(2)}, u32[]{:S(2)}) async-start(bf16[64,3,1]{1,2,0:T(2,128)(2,1)} %copy.218), calls=%async_computation.3 | async-start | bytes 65536 | tf_op jit(solution)/shard_map/all_to_all | solution.py:46
  109.9 9.6 collective-permute-start
  122.4 43.0 %all-to-all-start.4 = ((bf16[64,3,2048]{2,1,0:T(4,128)(2,1)}), bf16[64,3,2048]{2,1,0:T(4,128)(2,1)}, u32[]{:S(2)}, u32[]{:S(2)}) async-start(bf16[64,3,2048]{2,1,0:T(4,128)(2,1)} %copy.219), calls=%async_computation.4 | async-start | bytes 2097152 | tf_op jit(solution)/shard_map/all_to_all | solution.py:45
  178.0 24.5 %all-to-all-start.5 = ((bf16[64,3,2048]{2,1,0:T(4,128)(2,1)}), bf16[64,3,2048]{2,1,0:T(4,128)(2,1)}, u32[]{:S(2)}, u32[]{:S(2)}) async-start(bf16[64,3,2048]{2,1,0:T(4,128)(2,1)} %reshape.641), calls=%async_computation.5 | async-start | bytes 2097152 | tf_op jit(solution)/shard_map/all_to_all | solution.py:52
  205.4 23.7 %collective-permute-start.1 = (bf16[32,2048]{1,0:T(8,128)(2,1)S(1)}, bf16[32,2048]{1,0:T(8,128)(2,1)S(1)}, u32[]{:S(2)}, u32[]{:S(2)}) collective-permute-start(bf16[32,2048]{1,0:T(8,128)(2,1)S(1)} %get-tuple-element.841), channel_id=1, source_target_pairs={{0,8},{8,16},{16,24},{1,9},{9,17},{17,25},{2,10},{10,18},{18,26},{... | collective-permute-start | bytes 393224 | tf_op jit(solution)/shard_map/ppermute | solution.py:13
  224.3 16.5 %all-to-all-start.6 = ((bf16[64,3,1]{1,2,0:T(2,128)(2,1)}), bf16[64,3,1]{1,2,0:T(2,128)(2,1)S(1)}, u32[]{:S(2)}, u32[]{:S(2)}) async-start(bf16[64,3,1]{1,2,0:T(2,128)(2,1)} %copy.222), calls=%async_computation.6 | async-start | bytes 65536 | tf_op jit(solution)/shard_map/all_to_all | solution.py:46
  240.8 34.5 %all-to-all-start.7 = ((bf16[64,3,2048]{2,1,0:T(4,128)(2,1)}), bf16[64,3,2048]{2,1,0:T(4,128)(2,1)}, u32[]{:S(2)}, u32[]{:S(2)}) async-start(bf16[64,3,2048]{2,1,0:T(4,128)(2,1)} %copy.223), calls=%async_computation.7 | async-start | bytes 2097152 | tf_op jit(solution)/shard_map/all_to_all | solution.py:45
  287.7 31.1 %all-to-all-start.8 = ((bf16[64,3,2048]{2,1,0:T(4,128)(2,1)}), bf16[64,3,2048]{2,1,0:T(4,128)(2,1)}, u32[]{:S(2)}, u32[]{:S(2)}) async-start(bf16[64,3,2048]{2,1,0:T(4,128)(2,1)} %reshape.643), calls=%async_computation.8 | async-start | bytes 2097152 | tf_op jit(solution)/shard_map/all_to_all | solution.py:52
  321.7 11.8 collective-permute-start.2
  324.2 20.9 %all-to-all-start.9 = ((bf16[64,3,1]{1,2,0:T(2,128)(2,1)}), bf16[64,3,1]{1,2,0:T(2,128)(2,1)S(1)}, u32[]{:S(2)}, u32[]{:S(2)}) async-start(bf16[64,3,1]{1,2,0:T(2,128)(2,1)} %copy.226), calls=%async_computation.9 | async-start | bytes 65536 | tf_op jit(solution)/shard_map/all_to_all | solution.py:46
  345.1 32.7 %all-to-all-start.10 = ((bf16[64,3,2048]{2,1,0:T(4,128)(2,1)}), bf16[64,3,2048]{2,1,0:T(4,128)(2,1)}, u32[]{:S(2)}, u32[]{:S(2)}) async-start(bf16[64,3,2048]{2,1,0:T(4,128)(2,1)} %copy.227), calls=%async_computation.10 | async-start | bytes 2097152 | tf_op jit(solution)/shard_map/all_to_all | solution.py:45
  390.2 31.1 %all-to-all-start.11 = ((bf16[64,3,2048]{2,1,0:T(4,128)(2,1)}), bf16[64,3,2048]{2,1,0:T(4,128)(2,1)}, u32[]{:S(2)}, u32[]{:S(2)}) async-start(bf16[64,3,2048]{2,1,0:T(4,128)(2,1)} %reshape.645), calls=%async_computation.11 | async-start | bytes 2097152 | tf_op jit(solution)/shard_map/all_to_all | solution.py:52
  424.2 11.2 collective-permute-start.3
  426.2 20.7 %all-to-all-start.12 = ((bf16[64,3,1]{1,2,0:T(2,128)(2,1)}), bf16[64,3,1]{1,2,0:T(2,128)(2,1)S(1)}, u32[]{:S(2)}, u32[]{:S(2)}) async-start(bf16[64,3,1]{1,2,0:T(2,128)(2,1)} %copy.230), calls=%async_computation.12 | async-start | bytes 65536 | tf_op jit(solution)/shard_map/all_to_all | solution.py:46
  447.0 27.6 %all-to-all-start.13 = ((bf16[64,3,2048]{2,1,0:T(4,128)(2,1)}), bf16[64,3,2048]{2,1,0:T(4,128)(2,1)}, u32[]{:S(2)}, u32[]{:S(2)}) async-start(bf16[64,3,2048]{2,1,0:T(4,128)(2,1)} %copy.231), calls=%async_computation.13 | async-start | bytes 2097152 | tf_op jit(solution)/shard_map/all_to_all | solution.py:45
  479.9 30.7 %all-to-all-start.14 = ((bf16[64,3,2048]{2,1,0:T(4,128)(2,1)}), bf16[64,3,2048]{2,1,0:T(4,128)(2,1)}, u32[]{:S(2)}, u32[]{:S(2)}) async-start(bf16[64,3,2048]{2,1,0:T(4,128)(2,1)} %reshape.647), calls=%async_computation.14 | async-start | bytes 2097152 | tf_op jit(solution)/shard_map/all_to_all | solution.py:52
  513.5 11.1 collective-permute-start.4
  517.5 18.8 %all-to-all-start.15 = ((bf16[64,3,1]{1,2,0:T(2,128)(2,1)}), bf16[64,3,1]{1,2,0:T(2,128)(2,1)S(1)}, u32[]{:S(2)}, u32[]{:S(2)}) async-start(bf16[64,3,1]{1,2,0:T(2,128)(2,1)} %copy.234), calls=%async_computation.15 | async-start | bytes 65536 | tf_op jit(solution)/shard_map/all_to_all | solution.py:46
  536.3 28.2 %all-to-all-start.16 = ((bf16[64,3,2048]{2,1,0:T(4,128)(2,1)}), bf16[64,3,2048]{2,1,0:T(4,128)(2,1)}, u32[]{:S(2)}, u32[]{:S(2)}) async-start(bf16[64,3,2048]{2,1,0:T(4,128)(2,1)} %copy.235), calls=%async_computation.16 | async-start | bytes 2097152 | tf_op jit(solution)/shard_map/all_to_all | solution.py:45
  569.6 37.7 %all-to-all-start.17 = ((bf16[64,3,2048]{2,1,0:T(4,128)(2,1)}), bf16[64,3,2048]{2,1,0:T(4,128)(2,1)}, u32[]{:S(2)}, u32[]{:S(2)}) async-start(bf16[64,3,2048]{2,1,0:T(4,128)(2,1)} %reshape.649), calls=%async_computation.17 | async-start | bytes 2097152 | tf_op jit(solution)/shard_map/all_to_all | solution.py:52
  610.2 9.8 collective-permute-start.5
  612.5 19.1 %all-to-all-start.18 = ((bf16[64,3,1]{1,2,0:T(2,128)(2,1)}), bf16[64,3,1]{1,2,0:T(2,128)(2,1)S(1)}, u32[]{:S(2)}, u32[]{:S(2)}) async-start(bf16[64,3,1]{1,2,0:T(2,128)(2,1)} %copy.238), calls=%async_computation.18 | async-start | bytes 65536 | tf_op jit(solution)/shard_map/all_to_all | solution.py:46
  631.6 34.4 %all-to-all-start.19 = ((bf16[64,3,2048]{2,1,0:T(4,128)(2,1)}), bf16[64,3,2048]{2,1,0:T(4,128)(2,1)}, u32[]{:S(2)}, u32[]{:S(2)}) async-start(bf16[64,3,2048]{2,1,0:T(4,128)(2,1)} %copy.239), calls=%async_computation.19 | async-start | bytes 2097152 | tf_op jit(solution)/shard_map/all_to_all | solution.py:45
  666.0 24.4 %all-to-all-start.21 = ((bf16[64,3,2048]{2,1,0:T(4,128)(2,1)}), bf16[64,3,2048]{2,1,0:T(4,128)(2,1)}, u32[]{:S(2)}, u32[]{:S(2)}) async-start(bf16[64,3,2048]{2,1,0:T(4,128)(2,1)} %copy.242), calls=%async_computation.21 | async-start | bytes 2097152 | tf_op jit(solution)/shard_map/all_to_all | solution.py:56
  694.6 27.6 %all-to-all-start.22 = ((bf16[64,3,2048]{2,1,0:T(4,128)(2,1)}), bf16[64,3,2048]{2,1,0:T(4,128)(2,1)}, u32[]{:S(2)}, u32[]{:S(2)}) async-start(bf16[64,3,2048]{2,1,0:T(4,128)(2,1)} %reshape.654), calls=%async_computation.22 | async-start | bytes 2097152 | tf_op jit(solution)/shard_map/all_to_all | solution.py:60
  726.8 15.7 %collective-permute-start.6 = (bf16[32,2048]{1,0:T(8,128)(2,1)S(1)}, bf16[32,2048]{1,0:T(8,128)(2,1)S(1)}, u32[]{:S(2)}, u32[]{:S(2)}) collective-permute-start(bf16[32,2048]{1,0:T(8,128)(2,1)S(1)} %get-tuple-element.790), channel_id=1, source_target_pairs={{8,0},{16,8},{24,16},{9,1},{17,9},{25,17},{10,2},{18,10},{26,18},{... | collective-permute-start | bytes 393224 | tf_op jit(solution)/shard_map/ppermute | solution.py:13
  744.6 34.2 %all-to-all-start.23 = ((bf16[64,3,2048]{2,1,0:T(4,128)(2,1)}), bf16[64,3,2048]{2,1,0:T(4,128)(2,1)}, u32[]{:S(2)}, u32[]{:S(2)}) async-start(bf16[64,3,2048]{2,1,0:T(4,128)(2,1)} %copy.251), calls=%async_computation.23 | async-start | bytes 2097152 | tf_op jit(solution)/shard_map/all_to_all | solution.py:56
  783.1 24.3 %all-to-all-start.24 = ((bf16[64,3,2048]{2,1,0:T(4,128)(2,1)}), bf16[64,3,2048]{2,1,0:T(4,128)(2,1)}, u32[]{:S(2)}, u32[]{:S(2)}) async-start(bf16[64,3,2048]{2,1,0:T(4,128)(2,1)} %reshape.656), calls=%async_computation.24 | async-start | bytes 2097152 | tf_op jit(solution)/shard_map/all_to_all | solution.py:60
  811.5 12.8 collective-permute-start.7
  827.4 40.7 %all-to-all-start.25 = ((bf16[64,3,2048]{2,1,0:T(4,128)(2,1)}), bf16[64,3,2048]{2,1,0:T(4,128)(2,1)}, u32[]{:S(2)}, u32[]{:S(2)}) async-start(bf16[64,3,2048]{2,1,0:T(4,128)(2,1)} %copy.253), calls=%async_computation.25 | async-start | bytes 2097152 | tf_op jit(solution)/shard_map/all_to_all | solution.py:56
  872.5 24.3 %all-to-all-start.26 = ((bf16[64,3,2048]{2,1,0:T(4,128)(2,1)}), bf16[64,3,2048]{2,1,0:T(4,128)(2,1)}, u32[]{:S(2)}, u32[]{:S(2)}) async-start(bf16[64,3,2048]{2,1,0:T(4,128)(2,1)} %reshape.658), calls=%async_computation.26 | async-start | bytes 2097152 | tf_op jit(solution)/shard_map/all_to_all | solution.py:60
  900.9 18.4 %collective-permute-start.8 = (bf16[32,2048]{1,0:T(8,128)(2,1)S(1)}, bf16[32,2048]{1,0:T(8,128)(2,1)S(1)}, u32[]{:S(2)}, u32[]{:S(2)}) collective-permute-start(bf16[32,2048]{1,0:T(8,128)(2,1)S(1)} %get-tuple-element.786), channel_id=1, source_target_pairs={{8,0},{16,8},{24,16},{9,1},{17,9},{25,17},{10,2},{18,10},{26,18},{... | collective-permute-start | bytes 393224 | tf_op jit(solution)/shard_map/ppermute | solution.py:13
  922.4 36.3 %all-to-all-start.27 = ((bf16[64,3,2048]{2,1,0:T(4,128)(2,1)}), bf16[64,3,2048]{2,1,0:T(4,128)(2,1)}, u32[]{:S(2)}, u32[]{:S(2)}) async-start(bf16[64,3,2048]{2,1,0:T(4,128)(2,1)} %copy.255), calls=%async_computation.27 | async-start | bytes 2097152 | tf_op jit(solution)/shard_map/all_to_all | solution.py:56
  971.6 24.4 %all-to-all-start.28 = ((bf16[64,3,2048]{2,1,0:T(4,128)(2,1)}), bf16[64,3,2048]{2,1,0:T(4,128)(2,1)}, u32[]{:S(2)}, u32[]{:S(2)}) async-start(bf16[64,3,2048]{2,1,0:T(4,128)(2,1)} %reshape.660), calls=%async_computation.28 | async-start | bytes 2097152 | tf_op jit(solution)/shard_map/all_to_all | solution.py:60
  1000.1 9.3 collective-permute-start.9
  1012.4 36.3 %all-to-all-start.29 = ((bf16[64,3,2048]{2,1,0:T(4,128)(2,1)}), bf16[64,3,2048]{2,1,0:T(4,128)(2,1)}, u32[]{:S(2)}, u32[]{:S(2)}) async-start(bf16[64,3,2048]{2,1,0:T(4,128)(2,1)} %copy.257), calls=%async_computation.29 | async-start | bytes 2097152 | tf_op jit(solution)/shard_map/all_to_all | solution.py:56
  1061.6 24.4 %all-to-all-start.30 = ((bf16[64,3,2048]{2,1,0:T(4,128)(2,1)}), bf16[64,3,2048]{2,1,0:T(4,128)(2,1)}, u32[]{:S(2)}, u32[]{:S(2)}) async-start(bf16[64,3,2048]{2,1,0:T(4,128)(2,1)} %reshape.662), calls=%async_computation.30 | async-start | bytes 2097152 | tf_op jit(solution)/shard_map/all_to_all | solution.py:60
  1090.1 24.7 %collective-permute-start.10 = (bf16[32,2048]{1,0:T(8,128)(2,1)S(1)}, bf16[32,2048]{1,0:T(8,128)(2,1)S(1)}, u32[]{:S(2)}, u32[]{:S(2)}) collective-permute-start(bf16[32,2048]{1,0:T(8,128)(2,1)S(1)} %get-tuple-element.782), channel_id=1, source_target_pairs={{8,0},{16,8},{24,16},{9,1},{17,9},{25,17},{10,2},{18,10},{26,18},{... | collective-permute-start | bytes 393224 | tf_op jit(solution)/shard_map/ppermute | solution.py:13
  1117.9 33.7 %all-to-all-start.31 = ((bf16[64,3,2048]{2,1,0:T(4,128)(2,1)}), bf16[64,3,2048]{2,1,0:T(4,128)(2,1)}, u32[]{:S(2)}, u32[]{:S(2)}) async-start(bf16[64,3,2048]{2,1,0:T(4,128)(2,1)} %copy.259), calls=%async_computation.31 | async-start | bytes 2097152 | tf_op jit(solution)/shard_map/all_to_all | solution.py:56
  1164.6 33.5 %all-to-all-start.32 = ((bf16[64,3,2048]{2,1,0:T(4,128)(2,1)}), bf16[64,3,2048]{2,1,0:T(4,128)(2,1)}, u32[]{:S(2)}, u32[]{:S(2)}) async-start(bf16[64,3,2048]{2,1,0:T(4,128)(2,1)} %reshape.664), calls=%async_computation.32 | async-start | bytes 2097152 | tf_op jit(solution)/shard_map/all_to_all | solution.py:60
  1202.1 6.4 collective-permute-start.11
  1211.5 31.9 %all-to-all-start.33 = ((bf16[64,3,2048]{2,1,0:T(4,128)(2,1)}), bf16[64,3,2048]{2,1,0:T(4,128)(2,1)}, u32[]{:S(2)}, u32[]{:S(2)}) async-start(bf16[64,3,2048]{2,1,0:T(4,128)(2,1)} %copy.261), calls=%async_computation.33 | async-start | bytes 2097152 | tf_op jit(solution)/shard_map/all_to_all | solution.py:56
  1243.3 29.7 %all-to-all-start.20 = ((bf16[64,3,2048]{2,1,0:T(4,128)(2,1)}), bf16[64,3,2048]{2,1,0:T(4,128)(2,1)}, u32[]{:S(2)}, u32[]{:S(2)}) async-start(bf16[64,3,2048]{2,1,0:T(4,128)(2,1)} %reshape.651), calls=%async_computation.20 | async-start | bytes 2097152 | tf_op jit(solution)/shard_map/all_to_all | solution.py:52
  1273.1 27.2 %all-to-all-start.34 = ((bf16[64,3,2048]{2,1,0:T(4,128)(2,1)}), bf16[64,3,2048]{2,1,0:T(4,128)(2,1)S(1)}, u32[]{:S(2)}, u32[]{:S(2)}) async-start(bf16[64,3,2048]{2,1,0:T(4,128)(2,1)} %reshape.666), calls=%async_computation.34 | async-start | bytes 2097152 | tf_op jit(solution)/shard_map/all_to_all | solution.py:60
  1278.3 62.5 %copy-start.4 = (bf16[5,32,2048]{2,1,0:T(8,128)(2,1)S(1)}, bf16[5,32,2048]{2,1,0:T(8,128)(2,1)}, u32[]{:S(2)}) copy-start(bf16[5,32,2048]{2,1,0:T(8,128)(2,1)} %get-tuple-element.779) | copy-start | bytes 1966084
  (27 other events, 207.4 us)
